TPU v7x, 512 devices: a whole 4x4x16 slice. The times are simulated.
512 devices in a mesh: gx: 32 (over z, y_lo), row: 8 (over x, core), th: 2 (over y_hi).
Axes of the slice: x: 4, y: 4 (y_hi: 2, y_lo: 2; y = y_hi * 2 + y_lo), z: 16, core: 2. Of those that a mesh axis runs over, the one named last changes fastest.
Arguments:
- state: float32 [5, 1024, 128, 256], P(None, 'gx', 'row', 'th'), may hold values from -2 to 4, as said below
- adjoint_seed: float32 [5, 1024, 128, 256], P(None, 'gx', 'row', 'th'), may hold values from -6 to 6
- coef_x: float32 [9], replicated, may hold values from -1.75 to 1.75
- coef_r: float32 [9], replicated, may hold values from -1.75 to 1.75
- coef_t: float32 [9], replicated, may hold values from -1.75 to 1.75
- coef_filter: float32 [9], replicated, may hold values from -0.625 to 0.625
- metric: float32 [128], P('row'), may hold values from 0.5 to 2
Outputs:
- new_state: float32 [5, 1024, 128, 256], P(None, 'gx', 'row', 'th')
- adjoint_state: float32 [5, 1024, 128, 256], P(None, 'gx', 'row', 'th')
Inputs may be any that keep to these rules, and one draw needn't show every extreme that they name: `state`: component 0 (density) lies in [0.5, 1.5], components 1 to 3 (momenta) in [-2, 2], component 4 (total energy) in [2, 4].
All inputs are finite; a program needn't handle non-finite values.
Results may differ from a plain program's by a relative error of at most 0.0001.
Values sent between devices are 32-bit elements; how exact they have to be, the bound alone decides.
No kernel may reach another device: no remote copies, remote signals or barrier semaphores. Data moves between devices by JAX's collectives and lax.ppermute only.
A program may use at most 64 MiB of HBM per device.

v0:
```python
import jax
import jax.numpy as jnp
from jax import lax
from jax.experimental import pallas as pl
from jax.experimental.pallas import tpu as pltpu
from jax.sharding import PartitionSpec as P


DT = 0.1
GAM = 0.4
W = 4
TAPS = 9
C = 5
NX, NR, NT = 32, 16, 128
F32 = jnp.float32
BF16 = jnp.bfloat16
VM = pl.BlockSpec(memory_space=pltpu.VMEM)
SM = pl.BlockSpec(memory_space=pltpu.SMEM)
ANY = pl.BlockSpec(memory_space=pl.ANY)


def prims(q):
    inv = 1.0 / q[0]
    u, v, w = q[1] * inv, q[2] * inv, q[3] * inv
    p = GAM * (q[4] - 0.5 * (q[1] * u + q[2] * v + q[3] * w))
    return inv, u, v, w, p, q[4] + p


def flux_x(q, pr):
    _, u, _, _, p, h = pr
    return [q[1], q[1] * u + p, q[2] * u, q[3] * u, h * u]


def flux_r(q, pr):
    _, _, v, _, p, h = pr
    return [q[2], q[1] * v, q[2] * v + p, q[3] * v, h * v]


def flux_t(q, pr):
    _, _, _, w, p, h = pr
    return [q[3], q[1] * w, q[2] * w, q[3] * w + p, h * w]


def pull(q, pr, a, b, c):
    inv, u, v, w, _, h = pr
    ub = a[1] * q[1] + a[2] * q[2] + a[3] * q[3] + a[4] * h
    vb = b[1] * q[1] + b[2] * q[2] + b[3] * q[3] + b[4] * h
    wb = c[1] * q[1] + c[2] * q[2] + c[3] * q[3] + c[4] * h
    hb = a[4] * u + b[4] * v + c[4] * w
    pb = a[1] + b[2] + c[3] + hb
    s = (-0.5 * GAM) * pb
    ub = (ub + s * q[1]) * inv
    vb = (vb + s * q[2]) * inv
    wb = (wb + s * q[3]) * inv
    o1 = a[0] + (a[1] + s) * u + b[1] * v + c[1] * w + ub
    o2 = b[0] + a[2] * u + (b[2] + s) * v + c[2] * w + vb
    o3 = c[0] + a[3] * u + b[3] * v + (c[3] + s) * w + wb
    o4 = hb + GAM * pb
    o0 = -(ub * u + vb * v + wb * w)
    return [o0, o1, o2, o3, o4]


def pull_rt(q, pr, b, c):
    inv, u, v, w, _, h = pr
    hb = b[4] * v + c[4] * w
    pb = b[2] + c[3] + hb
    s = (-0.5 * GAM) * pb
    ub = s * u
    vb = (b[1] * q[1] + b[2] * q[2] + b[3] * q[3] + b[4] * h + s * q[2]) * inv
    wb = (c[1] * q[1] + c[2] * q[2] + c[3] * q[3] + c[4] * h + s * q[3]) * inv
    o1 = s * u + b[1] * v + c[1] * w + ub
    o2 = b[0] + (b[2] + s) * v + c[2] * w + vb
    o3 = c[0] + b[3] * v + (c[3] + s) * w + wb
    o4 = hb + GAM * pb
    o0 = -(ub * u + vb * v + wb * w)
    return [o0, o1, o2, o3, o4]


def iota(shape, dim):
    return lax.broadcasted_iota(jnp.int32, shape, dim)


def metric_tile(met):
    row = iota((NR, NT), 0)
    tile = jnp.zeros((NR, NT), F32)
    for r in range(NR):
        tile = jnp.where(row == r, met[r], tile)
    return tile


def parity(axis):
    return lax.axis_index(axis) % 2


def is_even(axis):
    return jnp.full((NR, NT), parity(axis), jnp.int32) == 0


def split(x):
    hi = x.astype(BF16)
    return hi, (x - hi.astype(F32)).astype(BF16)


def band(coef):
    offset = iota((NT, NT), 0) - iota((NT, NT), 1) + W
    mat = jnp.zeros((NT, NT), F32)
    for j in range(TAPS):
        mat = jnp.where(offset == j, coef[j], mat)
    return mat


def t_own(hi, lo, coef, out):
    bhi, blo = split(band(coef))
    mat = jnp.concatenate([bhi, bhi, blo], axis=0)
    step = 8
    for g in range(NX // step):
        h = hi[pl.ds(g * step, step)].reshape(step * C * NR, NT)
        l = lo[pl.ds(g * step, step)].reshape(step * C * NR, NT)
        total = jnp.dot(jnp.concatenate([h, l, h], axis=1), mat, preferred_element_type=F32)
        out[pl.ds(g * step, step)] = total.reshape(step, C, NR, NT)


def t_pack_coefs(coef):
    lane = iota((NR, NT), 1) % 8
    masks = {}
    for j in range(W):
        masks[j] = jnp.where((lane >= 4) & (lane < 8 - j), coef[j], 0.0)
    for j in range(W + 1, TAPS):
        masks[j] = jnp.where((lane >= 8 - j) & (lane < 4), coef[j], 0.0)
    return masks


def t_halo_packed(rims, masks):
    total = None
    for j, m in masks.items():
        term = m * pltpu.roll(rims, (4 - j) % NT, 1)
        total = term if total is None else total + term
    return total


def t_unpack(packed, k):
    lane = iota((NR, NT), 1)
    moved = pltpu.roll(packed, 124 - 8 * k, 1)
    return jnp.where((lane < 4) | (lane >= 124), moved, 0.0)


def t_pack_one(ref, at, field, k):
    moved = pltpu.roll(field, (8 * k + 4) % NT, 1)
    ref[at] = jnp.where(lane_block() == k, moved, ref[at])


def lane_block():
    return lax.shift_right_logical(iota((NR, NT), 1), 3)


def t_pack_into(ref, base, fields, xx, k):
    for c in range(C):
        t_pack_one(ref, base + 2 * c + xx, fields[c], k)


def r_pack(first, second, even):
    sub = iota((8, NT), 0)
    low = jnp.where(sub < 4, first[:8], pltpu.roll(second[:8], 4, 0))
    high = jnp.where(sub < 4, pltpu.roll(first[8:], 4, 0), second[8:])
    ev = even[:8]
    return jnp.where(ev, high, low), jnp.where(ev, low, high)


def r_coefs(coef):
    sub = iota((8, NT), 0)
    low = [jnp.where(sub < 4 - j, coef[j], 0.0) for j in range(W)]
    high = {j: jnp.where(sub >= 12 - j, coef[j], 0.0) for j in range(W + 1, TAPS)}
    return low, high


def r_halo(low, high, xlo, xhi, coefs):
    lo_c, hi_c = coefs
    top = None
    for j in range(W):
        shift = (8 - (4 * xlo + j)) % 8
        term = lo_c[j] * (pltpu.roll(low, shift, 0) if shift else low)
        top = term if top is None else top + term
    bottom = None
    for j in range(W + 1, TAPS):
        shift = (12 - j - 4 * xhi) % 8
        term = hi_c[j] * (pltpu.roll(high, shift, 0) if shift else high)
        bottom = term if bottom is None else bottom + term
    return jnp.concatenate([top, bottom], axis=0)


def x_taps(read, x, coef):
    total = None
    for j in range(TAPS):
        at = x + j - W
        if isinstance(x, int) and not 0 <= at < NX:
            continue
        term = coef[j] * read(at)
        total = term if total is None else total + term
    return total


def x_halo(planes, i, low, coef):
    total = None
    for j in range(TAPS):
        at = i + j if low else i + j - 8
        if not 0 <= at < W:
            continue
        term = coef[j] * planes[at]
        total = term if total is None else total + term
    return total


def over_planes(body):
    for x in range(W):
        body(x)

    def step(x, carry):
        body(x)
        return carry

    lax.fori_loop(W, NX - W, step, 0)
    for x in range(NX - W, NX):
        body(x)


def loop(lo, hi, body, unroll=1):
    def step(k, carry):
        body(k)
        return carry

    lax.fori_loop(lo, hi, step, 0, unroll=unroll)


def rim_starts():
    even = parity("gx") == 0
    return jnp.where(even, NX - W, 0), jnp.where(even, 0, NX - W)


def first(cf_hbm, state_hbm, seed_hbm, state, seed, prim, xe, xo, cf, sems):
    moves = [
        pltpu.make_async_copy(seed_hbm, seed, sems.at[0]),
        pltpu.make_async_copy(state_hbm, state, sems.at[1]),
        pltpu.make_async_copy(cf_hbm, cf, sems.at[2]),
    ]
    for move in moves:
        move.start()
    moves[2].wait()
    fc = [-cf[TAPS - 1 - j] for j in range(TAPS)]
    moves[0].wait()
    for side, base in enumerate((0, NX - W)):
        for i in range(W):
            for c in range(C):
                prim[side, c, i] = seed[c, base + i] + x_taps(lambda at: seed[c, at], base + i, fc)
    starts = rim_starts()
    even = parity("gx") == 0
    sides = jnp.where(even, 1, 0), jnp.where(even, 0, 1)
    moves[1].wait()
    for start, side, out in zip(starts, sides, (xe, xo)):
        for i in range(W):
            q = [state[c, start + i] for c in range(C)]
            f = flux_x(q, prims(q))
            for c in range(C):
                out[c, i] = f[c]
                out[C + c, i] = seed[c, start + i]
                out[2 * C + c, i] = prim[side, c, i]


def second(cf, met, state, seed, prim, plam, re, ro, th):
    fc = [-cf[TAPS - 1 - j] for j in range(TAPS)]
    mt = metric_tile(met)
    even = is_even("row")
    th[...] = jnp.zeros(th.shape, F32)
    for side, base in enumerate((0, NX - W)):
        for i in range(W):
            for c in range(C):
                plam[c, base + i] = prim[side, c, i]

    def plane(x):
        for c in range(C):
            plam[c, x] = seed[c, x] + x_taps(lambda at: seed[c, at], x, fc)

    loop(W, NX - W, plane, 2)

    def pair(k):
        keep = []
        for xx in range(2):
            q = [state[c, 2 * k + xx] for c in range(C)]
            pr = prims(q)
            keep.append(flux_r(q, pr))
            t_pack_into(th, 0, flux_t(q, pr), xx, k)
            t_pack_into(th, 2 * C, [mt * plam[c, 2 * k + xx] for c in range(C)], xx, k)
        for c in range(C):
            re[c, k], ro[c, k] = r_pack(keep[0][c], keep[1][c], even)
            at = NX // 2 + k
            re[c, at], ro[c, at] = r_pack(plam[c, 2 * k], plam[c, 2 * k + 1], even)

    loop(0, NX // 2, pair, 2)
    for n, k in enumerate(RIM_PAIRS):
        for c in range(C):
            at = NX + n
            re[c, at], ro[c, at] = r_pack(seed[c, 2 * k], seed[c, 2 * k + 1], even)
            for xx in range(2):
                t_pack_one(th, 4 * C + 2 * (n // 2) + xx, seed[c, 2 * k + xx], n % 2 + 2 * c)


def own(cx, cr, ct, met, state, psec, fx, fr, hi, lo, tt):
    mt = metric_tile(met)
    zero = jnp.zeros((8, NT), F32)

    def fill(x):
        q = [state[c, x] for c in range(C)]
        pr = prims(q)
        f, g, h = flux_x(q, pr), flux_r(q, pr), flux_t(q, pr)
        for c in range(C):
            fx[c, x] = f[c]
            fr[c, x, 0:8] = zero
            fr[c, x, 8:24] = g[c]
            fr[c, x, 24:32] = zero
            hi[x, c], lo[x, c] = split(h[c])

    loop(0, NX, fill)
    t_own(hi, lo, [-DT * ct[j] for j in range(TAPS)], tt)
    xc = [-DT * cx[j] for j in range(TAPS)]
    rc = [-DT * cr[j] for j in range(TAPS)]

    def plane(x):
        for c in range(C):
            acc = state[c, x] + mt * tt[x, c]
            acc += x_taps(lambda at: fx[c, at], x, xc)
            for j in range(TAPS):
                acc += rc[j] * fr[c, x, 4 + j : 20 + j]
            psec[c, x] = acc

    over_planes(plane)


def join(even_side, cx, cr, ct, cf, met, seed, psec, plam, x, re, ro, th, srim, lrim, lamh, x2):
    mt = metric_tile(met)
    ev8 = is_even("row")[:8]
    fc = [-cf[TAPS - 1 - j] for j in range(TAPS)]
    xc = [-DT * cx[j] for j in range(TAPS)]
    place = jnp.full((NR, NT), lax.axis_index("gx"), jnp.int32)
    has = place > 0, place < lax.axis_size("gx") - 1
    share = rt_share(cr, ct, mt, ev8, re, ro, th)

    def at_side(side):
        low, base = side == 0, (0, NX - W)[side]
        for c in range(C):
            flux = [x[c, i] for i in range(W)]
            seeds = [x[C + c, i] for i in range(W)]
            mine = [seed[c, base + i] for i in range(W)]
            both = []
            for p in range(2):
                both += share(c, RIM_PAIRS[2 * side + p])
            for i in range(W):
                value = psec[c, base + i] + x_halo(flux, i, low, xc) + both[i]
                srim[c, i] = value
                x2[W * c + i] = value
                lrim[c, i] = plam[c, base + i] + x_halo(seeds, i, low, fc)
                value = x[2 * C + c, i] + x_halo(mine, i, not low, fc)
                lamh[c, i] = jnp.where(has[side], value, 0.0)
            for eo, src in enumerate((re, ro)):
                for p in range(2):
                    x2[W * C + 2 * c + eo, 8 * p : 8 * p + 8] = src[c, NX + 2 * side + p]
        for xx in range(2):
            x2[(W + 2) * C + xx] = th[4 * C + 2 * side + xx]

    even = parity("gx") == 0
    pl.when(even)(lambda: at_side(even_side))
    pl.when(jnp.logical_not(even))(lambda: at_side(1 - even_side))


def join_e(*refs):
    join(1, *refs)


def join_o(*refs):
    join(0, *refs)


def rt_share(cr, ct, mt, ev8, re, ro, th):
    rc = r_coefs([-DT * cr[j] for j in range(TAPS)])
    tc = t_pack_coefs([-DT * ct[j] for j in range(TAPS)])
    packed = [[mt * t_halo_packed(th[2 * c + xx], tc) for xx in range(2)] for c in range(C)]

    def share(c, k):
        a, b = re[c, k], ro[c, k]
        low, high = jnp.where(ev8, b, a), jnp.where(ev8, a, b)
        return [r_halo(low, high, xx, xx, rc) + t_unpack(packed[c][xx], k) for xx in range(2)]

    return share


def finish(
    cx, cr, ct, cf, met, state, psec, plam, se, so, le, lo_, lhe, lho, re, ro, th,
    new, adj, nrim, arim, sec, lam, pk, lr, hi, lo, tt, nb, ab, sems,
):
    mt = metric_tile(met)
    evr = is_even("row")
    ev8 = evr[:8]
    rx = [-DT * cx[TAPS - 1 - j] for j in range(TAPS)]
    rr = [-DT * cr[TAPS - 1 - j] for j in range(TAPS)]
    rt = [-DT * ct[TAPS - 1 - j] for j in range(TAPS)]
    tc = t_pack_coefs(rt)
    evx = is_even("gx")

    def pick(side, e, o, c, i):
        mine, other = (o, e) if side == 0 else (e, o)
        return jnp.where(evx, mine[c, i], other[c, i])

    for c in range(C):
        for xx in range(2):
            pk[xx, c] = t_halo_packed(th[2 * C + 2 * c + xx], tc)
        for side, base in enumerate((0, NX - W)):
            for i in range(W):
                sec[c, base + i] = pick(side, se, so, c, i)
                lam[c, base + i] = pick(side, le, lo_, c, i)
    share = rt_share(cr, ct, mt, ev8, re, ro, th)

    def inner(k):
        for c in range(C):
            for xx, value in enumerate(share(c, k)):
                x = 2 * k + xx
                sec[c, x] = psec[c, x] + value
                lam[c, x] = plam[c, x]

    loop(2, 14, inner)

    def fill(k):
        for c in range(C):
            at = NX // 2 + k
            a, b = re[c, at], ro[c, at]
            low, high = jnp.where(ev8, b, a), jnp.where(ev8, a, b)
            for xx in range(2):
                x = 2 * k + xx
                value = lam[c, x]
                lr[c, x, 0:8] = low if xx else pltpu.roll(low, 4, 0)
                lr[c, x, 8:24] = value
                lr[c, x, 24:32] = pltpu.roll(high, 4, 0) if xx else high
                hi[x, c], lo[x, c] = split(mt * value)

    loop(0, NX // 2, fill)
    t_own(hi, lo, rt, tt)

    fcs = [cf[j] for j in range(TAPS)]

    def plane(x):
        q = [state[c, x] for c in range(C)]
        pr = prims(q)
        rim = isinstance(x, int)
        side, at = (0, x) if rim and x < W else (1, x - NX + W)
        a, b, g = [], [], []
        for c in range(C):
            acc = x_taps(lambda at: lam[c, at], x, rx)
            if rim:
                acc += x_halo([pick(side, lhe, lho, c, h) for h in range(W)], at, side == 0, rx)
            a.append(acc)
            acc = None
            for j in range(TAPS):
                term = rr[j] * lr[c, x, 4 + j : 20 + j]
                acc = term if acc is None else acc + term
            b.append(acc)
            g.append(tt[x, c] + t_unpack(pk[x % 2, c], x // 2))
        out = pull(q, pr, a, b, g)
        for c in range(C):
            av = lam[c, x] + out[c]
            nv = sec[c, x] - x_taps(lambda at: sec[c, at], x, fcs)
            if rim:
                arim[side, c, at], nrim[side, c, at] = av, nv
            else:
                ab[c, x - W], nb[c, x - W] = av, nv

    lax.fori_loop(W, NX - W, lambda x, carry: (plane(x), carry)[1], 0)
    inside = pl.ds(W, NX - 2 * W)
    moves = [
        pltpu.make_async_copy(ab, adj.at[:, inside], sems.at[0]),
        pltpu.make_async_copy(nb, new.at[:, inside], sems.at[1]),
    ]
    for move in moves:
        move.start()
    for x in (*range(W), *range(NX - W, NX)):
        plane(x)
    for move in moves:
        move.wait()


def edges(cr, ct, cf, met, state, xe2, xo2, nrim, arim, nin, ain, nout, aout, nb, ab, bs, gs, sems):
    mt = metric_tile(met)
    evx, evr = is_even("gx"), is_even("row")
    ev8 = evr[:8]
    sub = iota((8, NT), 0)
    fc = [-cf[TAPS - 1 - j] for j in range(TAPS)]
    fcs = [cf[j] for j in range(TAPS)]
    rc = r_coefs([-DT * cr[TAPS - 1 - j] for j in range(TAPS)])
    tc = t_pack_coefs([-DT * ct[TAPS - 1 - j] for j in range(TAPS)])
    starts = (0, NX - W)
    moves = []

    def put(buf, dst, side, slot):
        move = pltpu.make_async_copy(
            buf.at[side], dst.at[:, pl.ds(starts[side], W)], sems.at[slot + side]
        )
        move.start()
        moves.append(move)

    for side, at in enumerate(starts):
        low = side == 0
        mine, other = (xo2, xe2) if low else (xe2, xo2)

        def got(n):
            return jnp.where(evx, mine[n], other[n])

        for c in range(C):
            planes = [got(W * c + i) for i in range(W)]
            for i in range(W):
                nb[side, c, i] = nrim[side, c, i] - x_halo(planes, i, low, fcs)
        put(nb, nout, side, 0)
        turned = [t_halo_packed(got((W + 2) * C + xx), tc) for xx in range(2)]
        for c in range(C):
            one, two = got(W * C + 2 * c), got(W * C + 2 * c + 1)
            rows, lanes = [], []
            for p in range(2):
                e, o = one[8 * p : 8 * p + 8], two[8 * p : 8 * p + 8]
                lt, ht = jnp.where(ev8, o, e), jnp.where(ev8, e, o)
                rows.append(jnp.where(sub < 4, lt, pltpu.roll(ht, 4, 0)))
                rows.append(jnp.where(sub < 4, pltpu.roll(lt, 4, 0), ht))
                for xx in range(2):
                    lanes.append(mt * t_unpack(turned[xx], p + 2 * c))
            for i in range(W):
                row = x_halo(rows, i, low, fc)
                bs[c, i] = r_halo(row, row, 0, 1, rc)
                gs[c, i] = x_halo(lanes, i, low, fc)
        for i in range(W):
            q = [state[c, at + i] for c in range(C)]
            out = pull_rt(q, prims(q), [bs[c, i] for c in range(C)], [gs[c, i] for c in range(C)])
            for c in range(C):
                ab[side, c, i] = arim[side, c, i] + out[c]
        put(ab, aout, side, 2)
    for move in moves:
        move.wait()


def near(value):
    return pltpu.with_memory_space_constraint(value, pltpu.VMEM)


LIMIT = pltpu.CompilerParams(vmem_limit_bytes=24 << 20)
FULL = (C, NX, NR, NT)
XPAY = (3 * C, W, NR, NT)
XPAY2 = ((W + 2) * C + 2, NR, NT)
RPAY = (C, NX + 4, 8, NT)
TPAY = (4 * C + 4, NR, NT)
RIM = (2, C, W, NR, NT)
RIM_PAIRS = (0, 1, NX // 2 - 2, NX // 2 - 1)


def call(kernel, smem, vmem, outs, scratch=()):
    run = pl.pallas_call(
        kernel,
        in_specs=[SM] * len(smem) + [VM] * len(vmem),
        out_specs=[VM] * len(outs),
        out_shape=[pltpu.VMEM(s, F32) for s in outs],
        scratch_shapes=list(scratch),
        compiler_params=LIMIT,
    )
    return run(*smem, *[near(v) for v in vmem])


def swap(value, axis, odd):
    count = lax.axis_size(axis)
    pairs = []
    for i in range(odd, count - 1, 2):
        pairs += [(i, i + 1), (i + 1, i)]
    return lax.ppermute(value, axis, pairs)


def across(value):
    return lax.ppermute(value, "th", [(0, 1), (1, 0)])


SPLIT = [pltpu.VMEM((NX, C, NR, NT), BF16), pltpu.VMEM((NX, C, NR, NT), BF16), pltpu.VMEM((NX, C, NR, NT), F32)]
WIDE_R = pltpu.VMEM((C, NX, 32, NT), F32)


def shards(state, seed, cx, cr, ct, cf, met):
    shapes = [FULL, FULL, RIM, XPAY, XPAY]
    state, seed, prim, xe, xo = pl.pallas_call(
        first,
        in_specs=[pl.BlockSpec(memory_space=pltpu.HBM)] * 3,
        out_specs=[VM] * len(shapes),
        out_shape=[pltpu.VMEM(s, F32) for s in shapes],
        scratch_shapes=[pltpu.SMEM((TAPS,), F32), pltpu.SemaphoreType.DMA((3,))],
        name="first",
        compiler_params=LIMIT,
    )(*[pltpu.with_memory_space_constraint(v, pltpu.HBM) for v in (cf, state, seed)])
    xe = swap(xe, "gx", 0)
    xo = swap(xo, "gx", 1)
    plam, re, ro, th = call(second, [cf, met], [state, seed, prim], [FULL, RPAY, RPAY, TPAY])
    th = across(th)
    re = swap(re, "row", 0)
    ro = swap(ro, "row", 1)
    (psec,) = call(own, [cx, cr, ct, met], [state], [FULL], [pltpu.VMEM(FULL, F32), WIDE_R] + SPLIT)
    one = [(C, W, NR, NT)] * 3 + [XPAY2]
    near_args = [seed, psec, plam]
    se, le, lhe, xe2 = call(join_e, [cx, cr, ct, cf, met], near_args + [xe, re, ro, th], one)
    xe2 = swap(xe2, "gx", 0)
    so, lo, lho, xo2 = call(join_o, [cx, cr, ct, cf, met], near_args + [xo, re, ro, th], one)
    xo2 = swap(xo2, "gx", 1)
    full = pltpu.VMEM(FULL, F32)
    inner = pltpu.VMEM((C, NX - 2 * W, NR, NT), F32)
    whole = jax.ShapeDtypeStruct(FULL, F32)
    new, adj, nrim, arim = pl.pallas_call(
        finish,
        in_specs=[SM] * 5 + [VM] * 12,
        out_specs=[ANY, ANY, VM, VM],
        out_shape=[whole, whole, pltpu.VMEM(RIM, F32), pltpu.VMEM(RIM, F32)],
        scratch_shapes=[full, full, pltpu.VMEM((2, C, NR, NT), F32), WIDE_R]
        + SPLIT
        + [inner, inner, pltpu.SemaphoreType.DMA((2,))],
        name="finish",
        compiler_params=LIMIT,
    )(cx, cr, ct, cf, met, *map(near, (state, psec, plam, se, so, le, lo, lhe, lho, re, ro, th)))
    return pl.pallas_call(
        edges,
        in_specs=[SM] * 4 + [VM] * 5 + [ANY] * 2,
        out_specs=[ANY, ANY],
        out_shape=[whole, whole],
        scratch_shapes=[pltpu.VMEM(RIM, F32)] * 2
        + [pltpu.VMEM((C, W, NR, NT), F32)] * 2
        + [pltpu.SemaphoreType.DMA((4,))],
        input_output_aliases={9: 0, 10: 1},
        name="edges",
        compiler_params=LIMIT,
    )(cr, ct, cf, met, *map(near, (state, xe2, xo2, nrim, arim)), new, adj)


def solution(mesh):
    whole = P(None, "gx", "row", "th")

    return jax.shard_map(
        shards,
        mesh=mesh,
        in_specs=(whole, whole, P(), P(), P(), P(), P("row")),
        out_specs=(whole, whole),
        check_vma=False,
    )
```

profile of v0, /device:TPU:386, one launch (start us, length us, event | category | flops | bytes accessed | tf_op | source)
XLA Modules:
  0.0 61.9 jit_solution(9359320803468028184)
XLA Ops:
  0.6 0.0 copy-start.1
  0.6 0.0 copy-start
  0.7 1.8 %first.1 = (f32[5,32,16,128]{3,2,1,0:T(8,128)S(1)}, f32[5,32,16,128]{3,2,1,0:T(8,128)S(1)}, f32[2,5,4,16,128]{4,3,2,1,0:T(8,128)S(1)}, f32[15,4,16,128]{3,2,1,0:T(8,128)S(1)}, f32[15,4,16,128]{3,2,1,0:T(8,128)S(1)}) custom-call(f32[9]{0:T(128)} %cf.5, f32[5,32,16,128]{3,2,1,0:T(8,128)} %state_hbm.1, f32[5,32,16,128]{3,2,1,0:T(8,128)} %seed_hbm.1), custom_call_target="tpu_custom_call" | custom-call | tf_op jit(solution)/shard_map/first/pallas_call | solution.py:587
  2.5 0.0 copy-done.1
  2.5 0.0 copy-done
  2.5 0.0 copy-start.2
  2.5 0.0 copy-start.3
  2.5 0.0 copy-start.4
  2.5 2.7 %shard_map.87 = (f32[5,32,16,128]{3,2,1,0:T(8,128)S(1)}, f32[5,36,8,128]{3,2,1,0:T(8,128)S(1)}, f32[5,36,8,128]{3,2,1,0:T(8,128)S(1)}, f32[24,16,128]{2,1,0:T(8,128)S(1)}) custom-call(f32[9]{0:T(128)S(1)} %copy-done.1, f32[16]{0:T(128)S(1)} %copy-done, f32[5,32,16,128]{3,2,1,0:T(8,128)S(1)} %get-tuple-element.23.state, ...), custom_call_target="tpu_custom_call" | custom-call | tf_op jit(solution)/shard_map/pallas_call | solution.py:566
  5.2 1.9 %collective-permute-start.1 = (f32[5,36,8,128]{3,2,1,0:T(8,128)S(1)}, f32[5,36,8,128]{3,2,1,0:T(8,128)S(1)}, u32[]{:S(2)}, u32[]{:S(2)}) collective-permute-start(f32[5,36,8,128]{3,2,1,0:T(8,128)S(1)} %get-tuple-element.28), channel_id=1, source_target_pairs={{0,2},{2,0},{4,6},{6,4},{8,10},{10,8},{12,14},{14,12},{1,3},{3,1},... | collective-permute-start | bytes 2211848 | tf_op jit(solution)/shard_map/ppermute | solution.py:574
  7.1 2.5 %collective-permute-start.2 = (f32[5,36,8,128]{3,2,1,0:T(8,128)S(1)}, f32[5,36,8,128]{3,2,1,0:T(8,128)S(1)}, u32[]{:S(2)}, u32[]{:S(2)}) collective-permute-start(f32[5,36,8,128]{3,2,1,0:T(8,128)S(1)} %get-tuple-element.29), channel_id=1, source_target_pairs={{2,4},{4,2},{6,8},{8,6},{10,12},{12,10},{3,5},{5,3},{7,9},{9,7},{1... | collective-permute-start | bytes 2211848 | tf_op jit(solution)/shard_map/ppermute | solution.py:574
  9.7 3.5 %collective-permute-start = (f32[15,4,16,128]{3,2,1,0:T(8,128)S(1)}, f32[15,4,16,128]{3,2,1,0:T(8,128)S(1)}, u32[]{:S(2)}, u32[]{:S(2)}) collective-permute-start(f32[15,4,16,128]{3,2,1,0:T(8,128)S(1)} %get-tuple-element.27), channel_id=1, source_target_pairs={{0,16},{16,0},{32,48},{48,32},{64,80},{80,64},{96,112},{112,96},{1... | collective-permute-start | bytes 1474568 | tf_op jit(solution)/shard_map/ppermute | solution.py:574
  13.2 4.0 %collective-permute-start.5 = (f32[15,4,16,128]{3,2,1,0:T(8,128)S(1)}, f32[15,4,16,128]{3,2,1,0:T(8,128)S(1)}, u32[]{:S(2)}, u32[]{:S(2)}) collective-permute-start(f32[15,4,16,128]{3,2,1,0:T(8,128)S(1)} %get-tuple-element.32), channel_id=1, source_target_pairs={{16,32},{32,16},{48,64},{64,48},{80,96},{96,80},{112,128},{128,112... | collective-permute-start | bytes 1474568 | tf_op jit(solution)/shard_map/ppermute | solution.py:574
  17.2 5.1 %collective-permute-start.3 = (f32[24,16,128]{2,1,0:T(8,128)S(1)}, f32[24,16,128]{2,1,0:T(8,128)S(1)}, u32[]{:S(2)}, u32[]{:S(2)}) collective-permute-start(f32[24,16,128]{2,1,0:T(8,128)S(1)} %get-tuple-element.30), channel_id=1, source_target_pairs={{0,1},{1,0},{2,3},{3,2},{4,5},{5,4},{6,7},{7,6},{8,9},{9,8},{10,11... | collective-permute-start | bytes 589832 | tf_op jit(solution)/shard_map/ppermute | solution.py:578
  22.3 0.0 copy-done.2
  22.3 0.0 copy-done.3
  22.3 0.0 copy-done.4
  22.4 4.0 %shard_map.86.refs_6_.psec = f32[5,32,16,128]{3,2,1,0:T(8,128)S(1)} custom-call(f32[9]{0:T(128)S(1)} %copy-done.4, f32[9]{0:T(128)S(1)} %copy-done.2, f32[9]{0:T(128)S(1)} %copy-done.3, f32[16]{0:T(128)S(1)} %copy-done, f32[5,32,16,128]{3,2,1,0:T(8,128)S(1)} %get-tuple-element.23.state), custom_call_target="tpu_custom_call" | custom-call | tf_op jit(solution)/shard_map/pallas_call | solution.py:566
  26.3 16.5 %collective-permute-done.3.refs_11_.th = f32[24,16,128]{2,1,0:T(8,128)S(1)} collective-permute-done((f32[24,16,128]{2,1,0:T(8,128)S(1)}, f32[24,16,128]{2,1,0:T(8,128)S(1)}, u32[]{:S(2)}, u32[]{:S(2)}) %collective-permute-start.3) | collective-permute-done | bytes 196640 | tf_op jit(solution)/shard_map/ppermute | solution.py:578
  42.9 0.0 collective-permute-done.refs_8_
  42.9 0.0 collective-permute-done.1.refs_9_.re
  42.9 0.0 collective-permute-done.2.refs_10_.ro
  42.9 1.0 %shard_map.88 = (f32[5,4,16,128]{3,2,1,0:T(8,128)S(1)}, f32[5,4,16,128]{3,2,1,0:T(8,128)S(1)}, f32[5,4,16,128]{3,2,1,0:T(8,128)S(1)}, f32[32,16,128]{2,1,0:T(8,128)S(1)}) custom-call(f32[9]{0:T(128)S(1)} %copy-done.4, f32[9]{0:T(128)S(1)} %copy-done.2, f32[9]{0:T(128)S(1)} %copy-done.3, f32[9]{0:T(128)S(1)} %copy-done.1, f32[16]{0:T(128)S(1)} %copy-done, ...), custom_call_target="tpu_custom_call" | custom-call | tf_op jit(solution)/shard_map/pallas_call | solution.py:566
  43.9 2.0 %collective-permute-start.4 = (f32[32,16,128]{2,1,0:T(8,128)S(1)}, f32[32,16,128]{2,1,0:T(8,128)S(1)}, u32[]{:S(2)}, u32[]{:S(2)}) collective-permute-start(f32[32,16,128]{2,1,0:T(8,128)S(1)} %get-tuple-element.31), channel_id=1, source_target_pairs={{0,16},{16,0},{32,48},{48,32},{64,80},{80,64},{96,112},{112,96},{1... | collective-permute-start | bytes 786440 | tf_op jit(solution)/shard_map/ppermute | solution.py:574
  45.9 0.0 collective-permute-done.5.refs_8_
  46.0 1.0 %shard_map.89 = (f32[5,4,16,128]{3,2,1,0:T(8,128)S(1)}, f32[5,4,16,128]{3,2,1,0:T(8,128)S(1)}, f32[5,4,16,128]{3,2,1,0:T(8,128)S(1)}, f32[32,16,128]{2,1,0:T(8,128)S(1)}) custom-call(f32[9]{0:T(128)S(1)} %copy-done.4, f32[9]{0:T(128)S(1)} %copy-done.2, f32[9]{0:T(128)S(1)} %copy-done.3, f32[9]{0:T(128)S(1)} %copy-done.1, f32[16]{0:T(128)S(1)} %copy-done, ...), custom_call_target="tpu_custom_call" | custom-call | tf_op jit(solution)/shard_map/pallas_call | solution.py:566
  46.9 5.5 %collective-permute-start.6 = (f32[32,16,128]{2,1,0:T(8,128)S(1)}, f32[32,16,128]{2,1,0:T(8,128)S(1)}, u32[]{:S(2)}, u32[]{:S(2)}) collective-permute-start(f32[32,16,128]{2,1,0:T(8,128)S(1)} %get-tuple-element.33), channel_id=1, source_target_pairs={{16,32},{32,16},{48,64},{64,48},{80,96},{96,80},{112,128},{128,112... | collective-permute-start | bytes 786440 | tf_op jit(solution)/shard_map/ppermute | solution.py:574
  52.4 7.6 %finish.1 = (f32[5,32,16,128]{3,2,1,0:T(8,128)}, f32[5,32,16,128]{3,2,1,0:T(8,128)}, f32[2,5,4,16,128]{4,3,2,1,0:T(8,128)S(1)}, f32[2,5,4,16,128]{4,3,2,1,0:T(8,128)S(1)}) custom-call(f32[9]{0:T(128)S(1)} %copy-done.4, f32[9]{0:T(128)S(1)} %copy-done.2, f32[9]{0:T(128)S(1)} %copy-done.3, f32[9]{0:T(128)S(1)} %copy-done.1, f32[16]{0:T(128)S(1)} %copy-done, ...), custom_call_target="tpu_custom_call" | custom-call | tf_op jit(solution)/shard_map/finish/pallas_call | solution.py:612
  60.1 0.0 collective-permute-done.4.xe2
  60.1 0.0 collective-permute-done.6.xo2
  60.1 1.9 %edges.1 = (f32[5,32,16,128]{3,2,1,0:T(8,128)}, f32[5,32,16,128]{3,2,1,0:T(8,128)}) custom-call(f32[9]{0:T(128)S(1)} %copy-done.2, f32[9]{0:T(128)S(1)} %copy-done.3, f32[9]{0:T(128)S(1)} %copy-done.1, f32[16]{0:T(128)S(1)} %copy-done, f32[5,32,16,128]{3,2,1,0:T(8,128)S(1)} %get-tuple-element.23.state, ...), custom_call_target="tpu_custom_call", output_to_operand_aliasing={{0}: (9, {}), {1}: (10, {})} | custom-call | tf_op jit(solution)/shard_map/edges/pallas_call | solution.py:623
Async XLA Ops:
  0.6 1.9 %copy-start.1 = (f32[9]{0:T(128)S(1)}, f32[9]{0:T(128)}, u32[]{:S(2)}) copy-start(f32[9]{0:T(128)} %cf.5) | copy-start | bytes 112
  0.6 1.9 %copy-start = (f32[16]{0:T(128)S(1)}, f32[16]{0:T(128)}, u32[]{:S(2)}) copy-start(f32[16]{0:T(128)} %met.7) | copy-start | bytes 196
  2.5 19.8 %copy-start.2 = (f32[9]{0:T(128)S(1)}, f32[9]{0:T(128)}, u32[]{:S(2)}) copy-start(f32[9]{0:T(128)} %cr.5) | copy-start | bytes 112
  2.5 19.8 %copy-start.3 = (f32[9]{0:T(128)S(1)}, f32[9]{0:T(128)}, u32[]{:S(2)}) copy-start(f32[9]{0:T(128)} %ct.5) | copy-start | bytes 112
  2.5 19.8 %copy-start.4 = (f32[9]{0:T(128)S(1)}, f32[9]{0:T(128)}, u32[]{:S(2)}) copy-start(f32[9]{0:T(128)} %cx.3) | copy-start | bytes 112
  5.2 37.7 %collective-permute-start.1 = (f32[5,36,8,128]{3,2,1,0:T(8,128)S(1)}, f32[5,36,8,128]{3,2,1,0:T(8,128)S(1)}, u32[]{:S(2)}, u32[]{:S(2)}) collective-permute-start(f32[5,36,8,128]{3,2,1,0:T(8,128)S(1)} %get-tuple-element.28), channel_id=1, source_target_pairs={{0,2},{2,0},{4,6},{6,4},{8,10},{10,8},{12,14},{14,12},{1,3},{3,1},... | collective-permute-start | bytes 2211848 | tf_op jit(solution)/shard_map/ppermute | solution.py:574
  7.1 35.8 %collective-permute-start.2 = (f32[5,36,8,128]{3,2,1,0:T(8,128)S(1)}, f32[5,36,8,128]{3,2,1,0:T(8,128)S(1)}, u32[]{:S(2)}, u32[]{:S(2)}) collective-permute-start(f32[5,36,8,128]{3,2,1,0:T(8,128)S(1)} %get-tuple-element.29), channel_id=1, source_target_pairs={{2,4},{4,2},{6,8},{8,6},{10,12},{12,10},{3,5},{5,3},{7,9},{9,7},{1... | collective-permute-start | bytes 2211848 | tf_op jit(solution)/shard_map/ppermute | solution.py:574
  9.7 33.2 %collective-permute-start = (f32[15,4,16,128]{3,2,1,0:T(8,128)S(1)}, f32[15,4,16,128]{3,2,1,0:T(8,128)S(1)}, u32[]{:S(2)}, u32[]{:S(2)}) collective-permute-start(f32[15,4,16,128]{3,2,1,0:T(8,128)S(1)} %get-tuple-element.27), channel_id=1, source_target_pairs={{0,16},{16,0},{32,48},{48,32},{64,80},{80,64},{96,112},{112,96},{1... | collective-permute-start | bytes 1474568 | tf_op jit(solution)/shard_map/ppermute | solution.py:574
  13.2 32.8 %collective-permute-start.5 = (f32[15,4,16,128]{3,2,1,0:T(8,128)S(1)}, f32[15,4,16,128]{3,2,1,0:T(8,128)S(1)}, u32[]{:S(2)}, u32[]{:S(2)}) collective-permute-start(f32[15,4,16,128]{3,2,1,0:T(8,128)S(1)} %get-tuple-element.32), channel_id=1, source_target_pairs={{16,32},{32,16},{48,64},{64,48},{80,96},{96,80},{112,128},{128,112... | collective-permute-start | bytes 1474568 | tf_op jit(solution)/shard_map/ppermute | solution.py:574
  17.2 25.7 %collective-permute-start.3 = (f32[24,16,128]{2,1,0:T(8,128)S(1)}, f32[24,16,128]{2,1,0:T(8,128)S(1)}, u32[]{:S(2)}, u32[]{:S(2)}) collective-permute-start(f32[24,16,128]{2,1,0:T(8,128)S(1)} %get-tuple-element.30), channel_id=1, source_target_pairs={{0,1},{1,0},{2,3},{3,2},{4,5},{5,4},{6,7},{7,6},{8,9},{9,8},{10,11... | collective-permute-start | bytes 589832 | tf_op jit(solution)/shard_map/ppermute | solution.py:578
  43.9 16.2 %collective-permute-start.4 = (f32[32,16,128]{2,1,0:T(8,128)S(1)}, f32[32,16,128]{2,1,0:T(8,128)S(1)}, u32[]{:S(2)}, u32[]{:S(2)}) collective-permute-start(f32[32,16,128]{2,1,0:T(8,128)S(1)} %get-tuple-element.31), channel_id=1, source_target_pairs={{0,16},{16,0},{32,48},{48,32},{64,80},{80,64},{96,112},{112,96},{1... | collective-permute-start | bytes 786440 | tf_op jit(solution)/shard_map/ppermute | solution.py:574
  46.9 13.1 %collective-permute-start.6 = (f32[32,16,128]{2,1,0:T(8,128)S(1)}, f32[32,16,128]{2,1,0:T(8,128)S(1)}, u32[]{:S(2)}, u32[]{:S(2)}) collective-permute-start(f32[32,16,128]{2,1,0:T(8,128)S(1)} %get-tuple-element.33), channel_id=1, source_target_pairs={{16,32},{32,16},{48,64},{64,48},{80,96},{96,80},{112,128},{128,112... | collective-permute-start | bytes 786440 | tf_op jit(solution)/shard_map/ppermute | solution.py:574
where the time goes:
time: 62.2 us; the launch traced here: 61.9 us
  starting transfers between devices  24.6 us (40%)
  Pallas kernels  20 us (32%)
  waiting for transfers between devices  16.6 us (27%)
  between operations  0.84 us (1%)
    ppermute x6, starting transfers between devices, swap(): return lax.ppermute(value, axis, pairs)  19.5 us
    ppermute x1, waiting for transfers between devices, across(): return lax.ppermute(value, 'th', [(0, 1), (1, 0)])  16.5 us
    pallas_call x4, Pallas kernels, call(): return run(*smem, *[near(v) for v in vmem])  8.62 us
    pallas_call x1, Pallas kernels, shards(): pl.pallas_call(finish, in_specs=[SM] * 5 + [VM] * 12, out_specs=[ANY, ANY...  7.64 us
    ppermute x1, starting transfers between devices, across(): return lax.ppermute(value, 'th', [(0, 1), (1, 0)])  5.1 us
    pallas_call x1, Pallas kernels, shards(): pl.pallas_call(edges, in_specs=[SM] * 4 + [VM] * 5 + [ANY] * 2, out_specs...  1.87 us
    pallas_call x1, Pallas kernels, shards(): pl.pallas_call(first, in_specs=[pl.BlockSpec(memory_space=pltpu.HBM)] * 3...  1.83 us
  transfers between devices with their start and end apart: 7, of which 1 were waited for; matrix products, arithmetic and copies ran while one was open for 0% of the time, Pallas kernels for 22%

commit v1 on v0

--- a/solution.py
+++ b/solution.py
@@ -303,8 +303,7 @@
                 t_pack_one(th, 4 * C + 2 * (n // 2) + xx, seed[c, 2 * k + xx], n % 2 + 2 * c)
 
 
-def own(cx, cr, ct, met, state, psec, fx, fr, hi, lo, tt):
-    mt = metric_tile(met)
+def own_flux(ct, state, fx, fr, tt, hi, lo):
     zero = jnp.zeros((8, NT), F32)
 
     def fill(x):
@@ -320,6 +319,10 @@
 
     loop(0, NX, fill)
     t_own(hi, lo, [-DT * ct[j] for j in range(TAPS)], tt)
+
+
+def own(cx, cr, met, state, fx, fr, tt, psec):
+    mt = metric_tile(met)
     xc = [-DT * cx[j] for j in range(TAPS)]
     rc = [-DT * cr[j] for j in range(TAPS)]
 
@@ -599,7 +602,8 @@
     th = across(th)
     re = swap(re, "row", 0)
     ro = swap(ro, "row", 1)
-    (psec,) = call(own, [cx, cr, ct, met], [state], [FULL], [pltpu.VMEM(FULL, F32), WIDE_R] + SPLIT)
+    fx, fr, tt = call(own_flux, [ct], [state], [FULL, (C, NX, 32, NT), (NX, C, NR, NT)], SPLIT[:2])
+    (psec,) = call(own, [cx, cr, met], [state, fx, fr, tt], [FULL])
     one = [(C, W, NR, NT)] * 3 + [XPAY2]
     near_args = [seed, psec, plam]
     se, le, lhe, xe2 = call(join_e, [cx, cr, ct, cf, met], near_args + [xe, re, ro, th], one)

time: 62.2 us -> 65.1 us (1.047)
  the two profiles are of different devices: /device:TPU:386 before, /device:TPU:387 now
where the time goes in v1:
time: 65.1 us; the launch traced here: 64.8 us
  starting transfers between devices  22.6 us (35%)
  waiting for transfers between devices  20.7 us (32%)
  Pallas kernels  20.6 us (32%)
  between operations  0.83 us (1%)
    ppermute x6, starting transfers between devices, swap(): return lax.ppermute(value, axis, pairs)  18.1 us
    ppermute x1, waiting for transfers between devices, across(): return lax.ppermute(value, 'th', [(0, 1), (1, 0)])  17.3 us
    pallas_call x5, Pallas kernels, call(): return run(*smem, *[near(v) for v in vmem])  9.24 us
    pallas_call x1, Pallas kernels, shards(): pl.pallas_call(finish, in_specs=[SM] * 5 + [VM] * 12, out_specs=[ANY, ANY...  7.67 us
    ppermute x1, starting transfers between devices, across(): return lax.ppermute(value, 'th', [(0, 1), (1, 0)])  4.53 us
    ppermute x6, waiting for transfers between devices, swap(): return lax.ppermute(value, axis, pairs)  3.43 us
    pallas_call x1, Pallas kernels, shards(): pl.pallas_call(edges, in_specs=[SM] * 4 + [VM] * 5 + [ANY] * 2, out_specs...  1.87 us
    pallas_call x1, Pallas kernels, shards(): pl.pallas_call(first, in_specs=[pl.BlockSpec(memory_space=pltpu.HBM)] * 3...  1.83 us
  transfers between devices with their start and end apart: 7, of which 2 were waited for; matrix products, arithmetic and copies ran while one was open for 0% of the time, Pallas kernels for 22%

profile of v1, /device:TPU:387, one launch (start us, length us, event | category | flops | bytes accessed | tf_op | source)
XLA Modules:
  0.0 64.8 jit_solution(1774693519506332323)
XLA Ops:
  0.6 0.0 copy-start.1
  0.6 0.0 copy-start
  0.7 1.8 %first.1 = (f32[5,32,16,128]{3,2,1,0:T(8,128)S(1)}, f32[5,32,16,128]{3,2,1,0:T(8,128)S(1)}, f32[2,5,4,16,128]{4,3,2,1,0:T(8,128)S(1)}, f32[15,4,16,128]{3,2,1,0:T(8,128)S(1)}, f32[15,4,16,128]{3,2,1,0:T(8,128)S(1)}) custom-call(f32[9]{0:T(128)} %cf.5, f32[5,32,16,128]{3,2,1,0:T(8,128)} %state_hbm.1, f32[5,32,16,128]{3,2,1,0:T(8,128)} %seed_hbm.1), custom_call_target="tpu_custom_call" | custom-call | tf_op jit(solution)/shard_map/first/pallas_call | solution.py:590
  2.5 0.0 copy-done.1
  2.5 0.0 copy-done
  2.5 0.0 copy-start.3
  2.5 2.7 %shard_map.88 = (f32[5,32,16,128]{3,2,1,0:T(8,128)S(1)}, f32[5,36,8,128]{3,2,1,0:T(8,128)S(1)}, f32[5,36,8,128]{3,2,1,0:T(8,128)S(1)}, f32[24,16,128]{2,1,0:T(8,128)S(1)}) custom-call(f32[9]{0:T(128)S(1)} %copy-done.1, f32[16]{0:T(128)S(1)} %copy-done, f32[5,32,16,128]{3,2,1,0:T(8,128)S(1)} %get-tuple-element.26.state, ...), custom_call_target="tpu_custom_call" | custom-call | tf_op jit(solution)/shard_map/pallas_call | solution.py:569
  5.2 0.0 copy-start.2
  5.2 0.0 copy-start.4
  5.2 2.6 %collective-permute-start.1 = (f32[5,36,8,128]{3,2,1,0:T(8,128)S(1)}, f32[5,36,8,128]{3,2,1,0:T(8,128)S(1)}, u32[]{:S(2)}, u32[]{:S(2)}) collective-permute-start(f32[5,36,8,128]{3,2,1,0:T(8,128)S(1)} %get-tuple-element.34), channel_id=1, source_target_pairs={{0,2},{2,0},{4,6},{6,4},{8,10},{10,8},{12,14},{14,12},{1,3},{3,1},... | collective-permute-start | bytes 2211848 | tf_op jit(solution)/shard_map/ppermute | solution.py:577
  7.8 3.0 %collective-permute-start.2 = (f32[5,36,8,128]{3,2,1,0:T(8,128)S(1)}, f32[5,36,8,128]{3,2,1,0:T(8,128)S(1)}, u32[]{:S(2)}, u32[]{:S(2)}) collective-permute-start(f32[5,36,8,128]{3,2,1,0:T(8,128)S(1)} %get-tuple-element.35), channel_id=1, source_target_pairs={{2,4},{4,2},{6,8},{8,6},{10,12},{12,10},{3,5},{5,3},{7,9},{9,7},{1... | collective-permute-start | bytes 2211848 | tf_op jit(solution)/shard_map/ppermute | solution.py:577
  10.8 4.9 %collective-permute-start.5 = (f32[15,4,16,128]{3,2,1,0:T(8,128)S(1)}, f32[15,4,16,128]{3,2,1,0:T(8,128)S(1)}, u32[]{:S(2)}, u32[]{:S(2)}) collective-permute-start(f32[15,4,16,128]{3,2,1,0:T(8,128)S(1)} %get-tuple-element.38), channel_id=1, source_target_pairs={{16,32},{32,16},{48,64},{64,48},{80,96},{96,80},{112,128},{128,112... | collective-permute-start | bytes 1474568 | tf_op jit(solution)/shard_map/ppermute | solution.py:577
  15.7 1.9 %collective-permute-start = (f32[15,4,16,128]{3,2,1,0:T(8,128)S(1)}, f32[15,4,16,128]{3,2,1,0:T(8,128)S(1)}, u32[]{:S(2)}, u32[]{:S(2)}) collective-permute-start(f32[15,4,16,128]{3,2,1,0:T(8,128)S(1)} %get-tuple-element.33), channel_id=1, source_target_pairs={{0,16},{16,0},{32,48},{48,32},{64,80},{80,64},{96,112},{112,96},{1... | collective-permute-start | bytes 1474568 | tf_op jit(solution)/shard_map/ppermute | solution.py:577
  17.6 4.5 %collective-permute-start.3 = (f32[24,16,128]{2,1,0:T(8,128)S(1)}, f32[24,16,128]{2,1,0:T(8,128)S(1)}, u32[]{:S(2)}, u32[]{:S(2)}) collective-permute-start(f32[24,16,128]{2,1,0:T(8,128)S(1)} %get-tuple-element.36), channel_id=1, source_target_pairs={{0,1},{1,0},{2,3},{3,2},{4,5},{5,4},{6,7},{7,6},{8,9},{9,8},{10,11... | collective-permute-start | bytes 589832 | tf_op jit(solution)/shard_map/ppermute | solution.py:581
  22.2 0.0 copy-done.3
  22.2 2.0 %shard_map.86 = (f32[5,32,16,128]{3,2,1,0:T(8,128)S(1)}, f32[5,32,32,128]{3,2,1,0:T(8,128)S(1)}, f32[32,5,16,128]{3,2,1,0:T(8,128)S(1)}) custom-call(f32[9]{0:T(128)S(1)} %copy-done.3, f32[5,32,16,128]{3,2,1,0:T(8,128)S(1)} %get-tuple-element.26.state), custom_call_target="tpu_custom_call" | custom-call | tf_op jit(solution)/shard_map/pallas_call | solution.py:569
  24.2 0.0 copy-done.2
  24.2 0.0 copy-done.4
  24.2 2.6 %shard_map.87.refs_6_.psec = f32[5,32,16,128]{3,2,1,0:T(8,128)S(1)} custom-call(f32[9]{0:T(128)S(1)} %copy-done.4, f32[9]{0:T(128)S(1)} %copy-done.2, f32[16]{0:T(128)S(1)} %copy-done, f32[5,32,16,128]{3,2,1,0:T(8,128)S(1)} %get-tuple-element.26.state, f32[5,32,16,128]{3,2,1,0:T(8,128)S(1)} %get-tuple-element.28.fx, ...), custom_call_target="tpu_custom_call" | custom-call | tf_op jit(solution)/shard_map/pallas_call | solution.py:569
  26.8 17.3 %collective-permute-done.3.refs_11_.th = f32[24,16,128]{2,1,0:T(8,128)S(1)} collective-permute-done((f32[24,16,128]{2,1,0:T(8,128)S(1)}, f32[24,16,128]{2,1,0:T(8,128)S(1)}, u32[]{:S(2)}, u32[]{:S(2)}) %collective-permute-start.3) | collective-permute-done | bytes 196640 | tf_op jit(solution)/shard_map/ppermute | solution.py:581
  44.1 0.0 collective-permute-done.5.refs_8_
  44.1 0.0 collective-permute-done.1.refs_9_.re
  44.1 0.0 collective-permute-done.2.refs_10_.ro
  44.1 1.0 %shard_map.90 = (f32[5,4,16,128]{3,2,1,0:T(8,128)S(1)}, f32[5,4,16,128]{3,2,1,0:T(8,128)S(1)}, f32[5,4,16,128]{3,2,1,0:T(8,128)S(1)}, f32[32,16,128]{2,1,0:T(8,128)S(1)}) custom-call(f32[9]{0:T(128)S(1)} %copy-done.4, f32[9]{0:T(128)S(1)} %copy-done.2, f32[9]{0:T(128)S(1)} %copy-done.3, f32[9]{0:T(128)S(1)} %copy-done.1, f32[16]{0:T(128)S(1)} %copy-done, ...), custom_call_target="tpu_custom_call" | custom-call | tf_op jit(solution)/shard_map/pallas_call | solution.py:569
  45.1 3.4 %collective-permute-start.6 = (f32[32,16,128]{2,1,0:T(8,128)S(1)}, f32[32,16,128]{2,1,0:T(8,128)S(1)}, u32[]{:S(2)}, u32[]{:S(2)}) collective-permute-start(f32[32,16,128]{2,1,0:T(8,128)S(1)} %get-tuple-element.39), channel_id=1, source_target_pairs={{16,32},{32,16},{48,64},{64,48},{80,96},{96,80},{112,128},{128,112... | collective-permute-start | bytes 786440 | tf_op jit(solution)/shard_map/ppermute | solution.py:577
  48.5 0.0 collective-permute-done.refs_8_
  48.5 1.0 %shard_map.89 = (f32[5,4,16,128]{3,2,1,0:T(8,128)S(1)}, f32[5,4,16,128]{3,2,1,0:T(8,128)S(1)}, f32[5,4,16,128]{3,2,1,0:T(8,128)S(1)}, f32[32,16,128]{2,1,0:T(8,128)S(1)}) custom-call(f32[9]{0:T(128)S(1)} %copy-done.4, f32[9]{0:T(128)S(1)} %copy-done.2, f32[9]{0:T(128)S(1)} %copy-done.3, f32[9]{0:T(128)S(1)} %copy-done.1, f32[16]{0:T(128)S(1)} %copy-done, ...), custom_call_target="tpu_custom_call" | custom-call | tf_op jit(solution)/shard_map/pallas_call | solution.py:569
  49.5 2.3 %collective-permute-start.4 = (f32[32,16,128]{2,1,0:T(8,128)S(1)}, f32[32,16,128]{2,1,0:T(8,128)S(1)}, u32[]{:S(2)}, u32[]{:S(2)}) collective-permute-start(f32[32,16,128]{2,1,0:T(8,128)S(1)} %get-tuple-element.37), channel_id=1, source_target_pairs={{0,16},{16,0},{32,48},{48,32},{64,80},{80,64},{96,112},{112,96},{1... | collective-permute-start | bytes 786440 | tf_op jit(solution)/shard_map/ppermute | solution.py:577
  51.8 7.7 %finish.1 = (f32[5,32,16,128]{3,2,1,0:T(8,128)}, f32[5,32,16,128]{3,2,1,0:T(8,128)}, f32[2,5,4,16,128]{4,3,2,1,0:T(8,128)S(1)}, f32[2,5,4,16,128]{4,3,2,1,0:T(8,128)S(1)}) custom-call(f32[9]{0:T(128)S(1)} %copy-done.4, f32[9]{0:T(128)S(1)} %copy-done.2, f32[9]{0:T(128)S(1)} %copy-done.3, f32[9]{0:T(128)S(1)} %copy-done.1, f32[16]{0:T(128)S(1)} %copy-done, ...), custom_call_target="tpu_custom_call" | custom-call | tf_op jit(solution)/shard_map/finish/pallas_call | solution.py:616
  59.5 0.0 collective-permute-done.6.xo2
  59.5 3.4 %collective-permute-done.4.xe2 = f32[32,16,128]{2,1,0:T(8,128)S(1)} collective-permute-done((f32[32,16,128]{2,1,0:T(8,128)S(1)}, f32[32,16,128]{2,1,0:T(8,128)S(1)}, u32[]{:S(2)}, u32[]{:S(2)}) %collective-permute-start.4) | collective-permute-done | bytes 262176 | tf_op jit(solution)/shard_map/ppermute | solution.py:577
  62.9 1.9 %edges.1 = (f32[5,32,16,128]{3,2,1,0:T(8,128)}, f32[5,32,16,128]{3,2,1,0:T(8,128)}) custom-call(f32[9]{0:T(128)S(1)} %copy-done.2, f32[9]{0:T(128)S(1)} %copy-done.3, f32[9]{0:T(128)S(1)} %copy-done.1, f32[16]{0:T(128)S(1)} %copy-done, f32[5,32,16,128]{3,2,1,0:T(8,128)S(1)} %get-tuple-element.26.state, ...), custom_call_target="tpu_custom_call", output_to_operand_aliasing={{0}: (9, {}), {1}: (10, {})} | custom-call | tf_op jit(solution)/shard_map/edges/pallas_call | solution.py:627
Async XLA Ops:
  0.6 1.9 %copy-start.1 = (f32[9]{0:T(128)S(1)}, f32[9]{0:T(128)}, u32[]{:S(2)}) copy-start(f32[9]{0:T(128)} %cf.5) | copy-start | bytes 112
  0.6 1.9 %copy-start = (f32[16]{0:T(128)S(1)}, f32[16]{0:T(128)}, u32[]{:S(2)}) copy-start(f32[16]{0:T(128)} %met.7) | copy-start | bytes 196
  2.5 19.7 %copy-start.3 = (f32[9]{0:T(128)S(1)}, f32[9]{0:T(128)}, u32[]{:S(2)}) copy-start(f32[9]{0:T(128)} %ct.5) | copy-start | bytes 112
  5.2 19.0 %copy-start.2 = (f32[9]{0:T(128)S(1)}, f32[9]{0:T(128)}, u32[]{:S(2)}) copy-start(f32[9]{0:T(128)} %cr.5) | copy-start | bytes 112
  5.2 19.0 %copy-start.4 = (f32[9]{0:T(128)S(1)}, f32[9]{0:T(128)}, u32[]{:S(2)}) copy-start(f32[9]{0:T(128)} %cx.3) | copy-start | bytes 112
  5.2 38.8 %collective-permute-start.1 = (f32[5,36,8,128]{3,2,1,0:T(8,128)S(1)}, f32[5,36,8,128]{3,2,1,0:T(8,128)S(1)}, u32[]{:S(2)}, u32[]{:S(2)}) collective-permute-start(f32[5,36,8,128]{3,2,1,0:T(8,128)S(1)} %get-tuple-element.34), channel_id=1, source_target_pairs={{0,2},{2,0},{4,6},{6,4},{8,10},{10,8},{12,14},{14,12},{1,3},{3,1},... | collective-permute-start | bytes 2211848 | tf_op jit(solution)/shard_map/ppermute | solution.py:577
  7.8 36.3 %collective-permute-start.2 = (f32[5,36,8,128]{3,2,1,0:T(8,128)S(1)}, f32[5,36,8,128]{3,2,1,0:T(8,128)S(1)}, u32[]{:S(2)}, u32[]{:S(2)}) collective-permute-start(f32[5,36,8,128]{3,2,1,0:T(8,128)S(1)} %get-tuple-element.35), channel_id=1, source_target_pairs={{2,4},{4,2},{6,8},{8,6},{10,12},{12,10},{3,5},{5,3},{7,9},{9,7},{1... | collective-permute-start | bytes 2211848 | tf_op jit(solution)/shard_map/ppermute | solution.py:577
  10.8 33.2 %collective-permute-start.5 = (f32[15,4,16,128]{3,2,1,0:T(8,128)S(1)}, f32[15,4,16,128]{3,2,1,0:T(8,128)S(1)}, u32[]{:S(2)}, u32[]{:S(2)}) collective-permute-start(f32[15,4,16,128]{3,2,1,0:T(8,128)S(1)} %get-tuple-element.38), channel_id=1, source_target_pairs={{16,32},{32,16},{48,64},{64,48},{80,96},{96,80},{112,128},{128,112... | collective-permute-start | bytes 1474568 | tf_op jit(solution)/shard_map/ppermute | solution.py:577
  15.7 32.8 %collective-permute-start = (f32[15,4,16,128]{3,2,1,0:T(8,128)S(1)}, f32[15,4,16,128]{3,2,1,0:T(8,128)S(1)}, u32[]{:S(2)}, u32[]{:S(2)}) collective-permute-start(f32[15,4,16,128]{3,2,1,0:T(8,128)S(1)} %get-tuple-element.33), channel_id=1, source_target_pairs={{0,16},{16,0},{32,48},{48,32},{64,80},{80,64},{96,112},{112,96},{1... | collective-permute-start | bytes 1474568 | tf_op jit(solution)/shard_map/ppermute | solution.py:577
  17.6 26.4 %collective-permute-start.3 = (f32[24,16,128]{2,1,0:T(8,128)S(1)}, f32[24,16,128]{2,1,0:T(8,128)S(1)}, u32[]{:S(2)}, u32[]{:S(2)}) collective-permute-start(f32[24,16,128]{2,1,0:T(8,128)S(1)} %get-tuple-element.36), channel_id=1, source_target_pairs={{0,1},{1,0},{2,3},{3,2},{4,5},{5,4},{6,7},{7,6},{8,9},{9,8},{10,11... | collective-permute-start | bytes 589832 | tf_op jit(solution)/shard_map/ppermute | solution.py:581
  45.1 14.4 %collective-permute-start.6 = (f32[32,16,128]{2,1,0:T(8,128)S(1)}, f32[32,16,128]{2,1,0:T(8,128)S(1)}, u32[]{:S(2)}, u32[]{:S(2)}) collective-permute-start(f32[32,16,128]{2,1,0:T(8,128)S(1)} %get-tuple-element.39), channel_id=1, source_target_pairs={{16,32},{32,16},{48,64},{64,48},{80,96},{96,80},{112,128},{128,112... | collective-permute-start | bytes 786440 | tf_op jit(solution)/shard_map/ppermute | solution.py:577
  49.5 13.4 %collective-permute-start.4 = (f32[32,16,128]{2,1,0:T(8,128)S(1)}, f32[32,16,128]{2,1,0:T(8,128)S(1)}, u32[]{:S(2)}, u32[]{:S(2)}) collective-permute-start(f32[32,16,128]{2,1,0:T(8,128)S(1)} %get-tuple-element.37), channel_id=1, source_target_pairs={{0,16},{16,0},{32,48},{48,32},{64,80},{80,64},{96,112},{112,96},{1... | collective-permute-start | bytes 786440 | tf_op jit(solution)/shard_map/ppermute | solution.py:577
